TPU v7x, 32 devices: a whole 2x2x4 slice. The times are simulated.
32 devices in a mesh: row: 8 (over z, x), col: 4 (over y, core).
Axes of the slice: x: 2, y: 2, z: 4, core: 2. Of those that a mesh axis runs over, the one named last changes fastest.
Arguments:
- x_act: bfloat16 [512, 3072], P('col', 'row'), may hold values from -0.1875 to 0.1875
- grad_pre: bfloat16 [512, 8192], P('row', 'col'), may hold values from -6 to 6
- weight_blocks: bfloat16 [8, 4, 12, 128, 128], P('row', 'col'), may hold values from -0.1875 to 0.1875
- block_coord: int32 [8, 4, 12], P('row', 'col'), may hold values from -1 to 47, as said below
Outputs:
- grad_input: bfloat16 [512, 3072], P('col', 'row')
- grad_weight: bfloat16 [8, 4, 12, 128, 128], P('row', 'col')
Inputs may be any that keep to these rules, and one draw needn't show every extreme that they name: `block_coord`: in each tile the live slots come first and hold distinct local block numbers r * 16 + c (block row r, block column c of the tile) in ascending order; the remaining slots hold -1. Each tile has 1 to 12 live slots and some tile has all 12 live; values in the empty slots of weight_blocks are not read.
All inputs are finite; a program needn't handle non-finite values.
Results may differ from a plain program's by a relative error of at most 0.001.
Values may be sent and summed in bfloat16 or wider, within the bound.
A program may use at most 64 MiB of HBM per device.

v0:
```python
import jax
import jax.numpy as jnp
from jax import lax
from jax.sharding import PartitionSpec as P


def local(x_act, grad_pre, weight_blocks, block_coord):
    block_size = weight_blocks.shape[-1]
    slot_count = weight_blocks.shape[2]
    row_blocks = x_act.shape[1] // block_size
    col_blocks = grad_pre.shape[1] // block_size
    feature_width = x_act.shape[1]
    weights = weight_blocks[0, 0]
    own_coord = block_coord[0, 0]
    live_slot = own_coord >= 0
    safe_coord = jnp.where(live_slot, own_coord, 0)
    block_row = safe_coord // col_blocks
    block_col = safe_coord % col_blocks
    row_match = (
        block_row[None, :] == jnp.arange(row_blocks, dtype=jnp.int32)[:, None]
    ) & live_slot[None, :]
    weights_by_row = jnp.where(
        row_match[:, :, None, None], weights[None], jnp.zeros((), jnp.bfloat16)
    )
    x_all = lax.all_gather(x_act, "col", axis=0, tiled=True)

    def slots_of(panel_rows):
        row_count = panel_rows.shape[0]
        return jnp.take(panel_rows.reshape(row_count, col_blocks, block_size), block_col, axis=1)

    row_count = x_all.shape[0]
    x_slots = jnp.take(x_all.reshape(row_count, row_blocks, block_size), block_row, axis=1)
    w_sum = jnp.einsum(
        "nsa,nsb->sab",
        x_slots,
        slots_of(lax.all_gather(grad_pre, "row", axis=0, tiled=True)),
        preferred_element_type=jnp.float32,
    )
    grad_slots = slots_of(lax.all_gather(grad_pre, "row", axis=0, tiled=True))
    row_count = grad_slots.shape[0]
    x_term = jnp.einsum(
        "nsb,rsab->nra", grad_slots, weights_by_row, preferred_element_type=jnp.float32
    )
    x_partial = x_term.reshape(row_count, feature_width)
    input_sum = lax.psum_scatter(x_partial, "col", scatter_dimension=0, tiled=True)
    grad_input = input_sum.astype(jnp.bfloat16)
    grad_weight = jnp.where(live_slot[:, None, None], w_sum, jnp.float32(0.0)).astype(jnp.bfloat16)
    return (grad_input, grad_weight.reshape(1, 1, slot_count, block_size, block_size))


def solution(mesh):
    return jax.shard_map(
        local,
        mesh=mesh,
        in_specs=(
            P("col", "row"),
            P("row", "col"),
            P("row", "col", None, None, None),
            P("row", "col", None),
        ),
        out_specs=(P("col", "row"), P("row", "col", None, None, None)),
        check_vma=False,
    )
```

profile of v0, /device:TPU:0, one launch (start us, length us, event | category | flops | bytes accessed | tf_op | source)
XLA Modules:
  0.0 104.7 jit_solution(18392409356763328647)
XLA Ops:
  7.2 0.0 all-gather.2.cloned.1.call-start
  7.2 0.7 all-gather.2.cloned.1.call-update
  7.9 0.0 reduce-scatter.2.cloned.1.call-start
  7.9 0.7 compare_and_fusion.1
  8.7 53.3 %all-gather.2.cloned.1.call-done = bf16[512,2048]{1,0:T(8,128)(2,1)} async-done(((bf16[64,2048]{1,0:T(8,128)(2,1)}), bf16[512,2048]{1,0:T(8,128)(2,1)}) %all-gather.2.cloned.1.call-update) | async-done | bytes 2097168 | tf_op jit(solution)/shard_map/all_gather | solution.py:39
  61.9 3.9 %copy.17 = bf16[512,2048]{0,1:T(8,128)(2,1)} copy(bf16[512,2048]{1,0:T(8,128)(2,1)} %all-gather.2.cloned.1.call-done) | data formatting | bytes 4194304 | tf_op jit(solution)/shard_map/all_gather | solution.py:39
  65.9 3.0 %copy.18 = bf16[512,16,128]{2,0,1:T(8,128)(2,1)S(1)} copy(bf16[512,16,128]{0,2,1:T(8,128)(2,1)} %bitcast.48) | data formatting | bytes 4194304 | tf_op jit(solution)/shard_map/reshape | solution.py:29
  68.9 0.0 copy-start.3
  68.9 1.9 %gather_fusion.1 = bf16[12,512,128]{2,1,0:T(8,128)(2,1)} fusion(bf16[512,16,128]{2,0,1:T(8,128)(2,1)S(1)} %copy.18, s32[1024]{0:T(1024)S(1)} %pad_clamp_fusion.1), kind=kCustom, calls=%fused_computation.clone | custom fusion | bytes 3145776 | tf_op jit(solution)/shard_map/jit(_take)/gather | solution.py:29
  70.8 0.0 copy-done.3
  70.8 2.3 %fusion = f32[512,3,128,1]{0,2,3,1:T(8,128)S(1)} fusion(pred[3,12]{1,0:T(4,128)(4,1)S(1)} %fusion.27, bf16[12,512,128]{2,1,0:T(8,128)(2,1)} %gather_fusion.1, pred[12]{0:T(512)(128)(4,1)S(1)} %get-tuple-element.6, bf16[12,128,128]{2,1,0:T(8,128)(2,1)S(1)} %bitcast.51), kind=kOutput, calls=%fused_computation.2 | convolution fusion | flops 605356032 | bytes 2752560 | tf_op jit(solution)/shard_map/nsb,rsab->nra/dot_general | solution.py:41
  73.1 0.0 copy-start.1
  73.1 0.0 copy-start.2
  73.2 1.1 %copy.19 = f32[512,384]{1,0:T(8,128)} copy(f32[512,384]{0,1:T(8,128)S(1)} %bitcast.50) | data formatting | bytes 1572864 | tf_op jit(solution)/shard_map/reshape | solution.py:44
  74.3 0.0 reduce-scatter.2.cloned.1.call-update
  74.3 0.0 copy-done.1
  74.3 0.1 copy.20
  74.5 6.5 %all_gather.8 = bf16[512,384]{0,1:T(8,128)(2,1)S(1)} all-gather(bf16[128,384]{0,1:T(8,128)(2,1)S(1)} %copy.20), channel_id=1, replica_groups=mesh['row'=8,'col'=4] {'col'}, dimensions={0}, use_global_device_ids=true | all-gather | bytes 491520 | tf_op jit(solution)/shard_map/all_gather | solution.py:25
  80.9 0.2 copy.21
  81.2 0.8 gather_fusion
  82.1 0.6 copy-done
  82.6 1.5 %fusion.17 = bf16[1,1,12,128,128]{4,3,2,1,0:T(8,128)(2,1)} fusion(bf16[12,512,128]{2,1,0:T(8,128)(2,1)S(1)} %gather_fusion, pred[12]{0:T(512)(128)(4,1)S(1)} %get-tuple-element.3, bf16[12,512,128]{2,1,0:T(8,128)(2,1)S(1)} %copy-done, pred[12]{0:T(512)(128)(4,1)S(1)} %get-tuple-element.6, pred[12]{0:T(512)(128)(4,1)S(1)} %get-tuple-element.8), kind=kOutput, calls=%fused_computation.12 | convolution fusion | flops 203292672 | bytes 3538980 | tf_op jit(solution)/shard_map/nsa,nsb->sab/dot_general | solution.py:33
  84.2 12.1 %reduce-scatter.2.cloned.1.call-done = f32[128,384]{1,0:T(8,128)} async-done(((f32[512,384]{1,0:T(8,128)}), f32[128,384]{1,0:T(8,128)}) %reduce-scatter.2.cloned.1.call-update) | async-done | bytes 196624 | tf_op jit(solution)/shard_map/reduce_scatter | solution.py:45
  96.3 1.6 %convert_element_type.6 = bf16[128,384]{1,0:T(8,128)(2,1)} convert(f32[128,384]{1,0:T(8,128)} %reduce-scatter.2.cloned.1.call-done) | non-fusion elementwise | flops 49152 | bytes 294912 | tf_op jit(solution)/shard_map/convert_element_type | solution.py:46
  (7 shorter events, 0.0 us)
Async XLA Ops:
  7.2 54.8 %all-gather.2.cloned.1.call-start = ((), (), s32[]{:S(2)}) async-start(), calls=%async_computation.1 | async-start | bytes 2359296 | tf_op jit(solution)/shard_map/all_gather | solution.py:39
  7.9 88.4 %reduce-scatter.2.cloned.1.call-start = ((), (), s32[]{:S(2)}) async-start(), calls=%async_computation.2 | async-start | bytes 983040 | tf_op jit(solution)/shard_map/reduce_scatter | solution.py:45
  68.9 2.0 %copy-start.3 = (bf16[1,1,12,128,128]{4,3,2,1,0:T(8,128)(2,1)S(1)}, bf16[1,1,12,128,128]{4,3,2,1,0:T(8,128)(2,1)}, u32[]{:S(2)}) copy-start(bf16[1,1,12,128,128]{4,3,2,1,0:T(8,128)(2,1)} %param.8) | copy-start | bytes 1179652
  73.1 1.2 %copy-start.1 = (bf16[128,384]{1,0:T(8,128)(2,1)S(1)}, bf16[128,384]{1,0:T(8,128)(2,1)}, u32[]{:S(2)}) copy-start(bf16[128,384]{1,0:T(8,128)(2,1)} %param.6) | copy-start | bytes 294916
  73.1 8.0 %copy-start.2 = (s32[1,1,12]{2,1,0:T(1,128)S(1)}, s32[1,1,12]{2,1,0:T(1,128)}, u32[]{:S(2)}) copy-start(s32[1,1,12]{2,1,0:T(1,128)} %param.9) | copy-start | bytes 148
  81.2 1.4 %copy-start = (bf16[12,512,128]{2,1,0:T(8,128)(2,1)S(1)}, bf16[12,512,128]{2,1,0:T(8,128)(2,1)}, u32[]{:S(2)}) copy-start(bf16[12,512,128]{2,1,0:T(8,128)(2,1)} %gather_fusion.1) | copy-start | bytes 4718596
Sparse Core Ops, SparseCore 0:
  10.1 51.7 all-gather.1
  74.5 21.7 reduce-scatter.1
where the time goes:
time: 105 us
  waiting for transfers between devices  66.1 us (63%)
  between operations  14.2 us (14%)
  local copies, waits for them, and re-layouts  11.8 us (11%)
  blocking collectives  6.47 us (6%)
  matrix products  3.79 us (4%)
  other arithmetic  2.29 us (2%)
    all_gather x1, waiting for transfers between devices, local(): grad_slots = slots_of(lax.all_gather(grad_pre, 'row', axis=0, tiled=True))  53.3 us
    reduce_scatter x1, waiting for transfers between devices, local(): lax.psum_scatter(x_partial, 'col', scatter_dimension=0, tiled=True)  12.1 us
    all_gather x1, blocking collectives, local(): x_all = lax.all_gather(x_act, 'col', axis=0, tiled=True)  6.47 us
    all_gather x1, local copies, waits for them, and re-layouts, local(): grad_slots = slots_of(lax.all_gather(grad_pre, 'row', axis=0, tiled=True))  3.91 us
    reshape x1, local copies, waits for them, and re-layouts, slots_of(): panel_rows.reshape(row_count, col_blocks, block_size)  3.03 us
    dot_general x1, matrix products, local(): jnp.einsum('nsb,rsab->nra', grad_slots, weights_by_row, preferred_element...  2.28 us
  transfers between devices with their start and end apart: 2, of which 2 were waited for; matrix products, arithmetic and copies ran while one was open for 3% of the time, Pallas kernels for 0%

commit v1 on v0

v1 whole, which is shorter than its diff:
```python
import functools

import jax
import jax.numpy as jnp
from jax import lax
from jax.experimental import pallas as pl
from jax.experimental.pallas import tpu as pltpu
from jax.sharding import PartitionSpec as P

MESH = pl.DeviceIdType.MESH
CORES = 2
CHUNKS = 2
F32 = jnp.float32
BF16 = jnp.bfloat16


def either(a, b):
    if a is True or b is True:
        return True
    if a is False:
        return b
    if b is False:
        return a
    return jnp.logical_or(a, b)


def both(a, b):
    if a is False or b is False:
        return False
    if a is True:
        return b
    if b is True:
        return a
    return jnp.logical_and(a, b)


def negate(a):
    return (not a) if isinstance(a, bool) else jnp.logical_not(a)


def when(cond, body):
    if cond is True:
        body()
    elif cond is not False:
        pl.when(cond)(body)


def kernel(
    rows, cols, coord_ref, x_ref, g_ref, w_ref, gi_ref, gw_ref,
    g_all, x_all, x_t, w_own, w_t, dense, part, pair_in, y_in,
    local_sem, g_send, g_recv, x_send, x_recv, pair_send, pair_recv, y_send, y_recv,
):
    hi_n = 4 if rows % 4 == 0 else 1
    lo_n = rows // hi_n
    y_n = cols // CORES
    slots, blk = w_own.shape[0], w_own.shape[1]
    tokens = g_all.shape[1]
    step_rows = tokens // CHUNKS
    row_blocks = x_t.shape[0] // blk
    col_blocks = g_all.shape[2] // blk
    per_group = rows // cols

    row = lax.axis_index("row")
    col = lax.axis_index("col")
    hi, lo = lax.div(row, lo_n), lax.rem(row, lo_n)
    y, core = lax.div(col, CORES), lax.rem(col, CORES)
    sibling = (row, y * CORES + (1 - core))
    own = row

    def peer_y(dist):
        return lax.rem(y + dist, y_n)

    directions = (
        (hi < hi_n - 1, (row + lo_n, col)),
        (hi > 0, (row - lo_n, col)),
        (lo < lo_n - 1, (row + 1, col)),
        (lo > 0, (row - 1, col)),
    )

    own_g = pltpu.make_async_copy(g_ref, g_all.at[own], local_sem.at[0])
    own_x = pltpu.make_async_copy(x_ref, x_all.at[col], local_sem.at[1])
    own_w = pltpu.make_async_copy(w_ref, w_own, local_sem.at[2])
    own_w.start()
    own_g.start()
    own_x.start()

    barrier = pltpu.get_barrier_semaphore()
    count = jnp.int32(y_n)
    for there, device in directions:
        count = count + there.astype(jnp.int32)

        def greet(device=device):
            pl.semaphore_signal(barrier, inc=1, device_id=device, device_id_type=MESH)

        when(there, greet)
    pl.semaphore_signal(barrier, inc=1, device_id=sibling, device_id_type=MESH)
    for dist in range(1, y_n):
        pl.semaphore_signal(
            barrier, inc=1, device_id=(row, peer_y(dist) * CORES + core), device_id_type=MESH
        )
    pl.semaphore_wait(barrier, count)

    def g_copy(block, chunk, direction, from_input=False):
        span = pl.ds(chunk * step_rows, step_rows)
        there = g_all.at[block, span]
        return pltpu.make_async_remote_copy(
            src_ref=g_ref.at[span] if from_input else there,
            dst_ref=there,
            send_sem=g_send.at[direction, block, chunk],
            recv_sem=g_recv.at[block, chunk],
            device_id=directions[direction][1],
            device_id_type=MESH,
        )

    def sends(dh, dl, chunk):
        origin = hi + dh
        swapped = False
        if chunk == CHUNKS - 1:
            swapped = jnp.logical_or(origin == 0, origin == hi_n - 1)
        along_hi = either(swapped, dl == 0)
        along_lo = either(negate(swapped), dh == 0)
        conds = (
            both(along_hi, dh <= 0), both(along_hi, dh >= 0),
            both(along_lo, dl <= 0), both(along_lo, dl >= 0),
        )
        return [both(cond, directions[n][0]) for n, cond in enumerate(conds)]

    def valid(dh, dl):
        cond = True
        if dh > 0:
            cond = both(cond, hi + dh < hi_n)
        if dh < 0:
            cond = both(cond, hi + dh >= 0)
        if dl > 0:
            cond = both(cond, lo + dl < lo_n)
        if dl < 0:
            cond = both(cond, lo + dl >= 0)
        return cond

    def block_of(dh, dl):
        return row + (dh * lo_n + dl)

    def forward(dh, dl, chunk):
        for n, cond in enumerate(sends(dh, dl, chunk)):
            when(cond, lambda n=n: g_copy(block_of(dh, dl), chunk, n, dh == 0 and dl == 0).start())

    def arrive(dh, dl, chunk):
        def body():
            g_copy(block_of(dh, dl), chunk, 0).wait_recv()
            forward(dh, dl, chunk)

        when(valid(dh, dl), body)

    def drain(dh, dl, chunk):
        def body():
            for n, cond in enumerate(sends(dh, dl, chunk)):
                when(cond, lambda n=n: g_copy(block_of(dh, dl), chunk, n, dh == 0 and dl == 0).wait_send())

        when(valid(dh, dl), body)

    def x_copy(index, group, device, from_input=False):
        return pltpu.make_async_remote_copy(
            src_ref=x_ref if from_input else x_all.at[group],
            dst_ref=x_all.at[group],
            send_sem=x_send.at[index],
            recv_sem=x_recv.at[group],
            device_id=device,
            device_id_type=MESH,
        )

    def x_to_y(dist):
        return x_copy(dist, col, (row, peer_y(dist) * CORES + core), True)

    def x_to_sibling(dist):
        return x_copy(y_n + dist, peer_y(dist) * CORES + core, sibling, dist == 0)

    def x_from_sibling(dist):
        return x_copy(0, peer_y(dist) * CORES + (1 - core), sibling)

    def group_of(block):
        return lax.div(block, per_group)

    def mine(block):
        return lax.rem(group_of(block), CORES) == core

    def pair_copy(block):
        return pltpu.make_async_remote_copy(
            src_ref=part.at[block],
            dst_ref=pair_in.at[block],
            send_sem=pair_send.at[block],
            recv_sem=pair_recv.at[block],
            device_id=sibling,
            device_id_type=MESH,
        )

    def y_copy(block):
        sub = lax.rem(block, per_group)
        return pltpu.make_async_remote_copy(
            src_ref=part.at[block],
            dst_ref=y_in.at[y, sub],
            send_sem=y_send.at[block],
            recv_sem=y_recv.at[y, sub],
            device_id=(row, group_of(block)),
            device_id_type=MESH,
        )

    def compute(dh, dl):
        def body():
            block = block_of(dh, dl)
            part[block] = jnp.dot(g_all[block], dense[...], preferred_element_type=F32)
            when(negate(mine(block)), lambda: pair_copy(block).start())

        when(valid(dh, dl), body)

    def finish(dh, dl):
        def body():
            block = block_of(dh, dl)

            def reduce():
                pair_copy(block).wait_recv()
                part[block] = part[block] + pair_in[block]
                when(group_of(block) != col, lambda: y_copy(block).start())

            when(mine(block), reduce)

        when(valid(dh, dl), body)

    for chunk in range(CHUNKS):
        forward(0, 0, chunk)
    for dist in range(1, y_n):
        x_to_y(dist).start()
    x_to_sibling(0).start()

    own_w.wait()

    def turn(s, carry):
        w_t[s] = w_own[s].T
        return carry

    lax.fori_loop(0, slots, turn, 0)

    def spread(c, carry):
        for r in range(row_blocks):
            total = jnp.zeros((blk, blk), BF16)
            for s in range(slots):
                hit = (coord_ref[0, s] == r * col_blocks + c).astype(F32)
                total = total + w_t[s] * jnp.full((blk, blk), hit, F32).astype(BF16)
            dense[pl.ds(pl.multiple_of(c * blk, blk), blk), r * blk:(r + 1) * blk] = total
        return carry

    lax.fori_loop(0, col_blocks, spread, 0)

    own_g.wait()
    own_x.wait()
    compute(0, 0)

    steps = []
    for t in range(1, hi_n + lo_n - 1):
        step = []
        for far in range(min(t, hi_n - 1), -1, -1):
            side = t - far
            if side >= lo_n:
                continue
            for dh in sorted({far, -far}):
                for dl in sorted({side, -side}):
                    step.append((dh, dl))
        steps.append(step)

    pending = [(0, 0)]
    for index, step in enumerate(steps):
        for chunk in range(CHUNKS):
            for dh, dl in step:
                arrive(dh, dl, chunk)
        if index == 0:
            for dist in range(1, y_n):
                x_copy(0, peer_y(dist) * CORES + core, sibling).wait_recv()
                x_to_sibling(dist).start()
        for dh, dl in step:
            compute(dh, dl)
        if index < len(steps) - 1:
            for dh, dl in pending:
                finish(dh, dl)
            pending = []
        pending = pending + step
        if index == min(1, len(steps) - 1):
            for dist in range(y_n):
                x_from_sibling(dist).wait_recv()
            for r in range(row_blocks):
                for group in range(cols):
                    span = x_all.shape[1]
                    x_t[r * blk:(r + 1) * blk, group * span:(group + 1) * span] = x_all[
                        group, :, r * blk:(r + 1) * blk
                    ].T

    pair_width = 2 * blk

    def weight_grads(n, carry):
        start = pl.multiple_of(n * pair_width, pair_width)
        g_cols = g_all[:, :, pl.ds(start, pair_width)].reshape(rows * tokens, pair_width)
        total = jnp.dot(x_t[...], g_cols, preferred_element_type=F32).astype(BF16)
        for r in range(row_blocks):
            for c in range(2):
                gw_ref[r * col_blocks + 2 * n + c] = total[
                    r * blk:(r + 1) * blk, c * blk:(c + 1) * blk
                ]
        return carry

    pairs = col_blocks // 2
    lax.fori_loop(0, pairs // 2, weight_grads, 0)
    for dh, dl in pending:
        finish(dh, dl)
    lax.fori_loop(pairs // 2, pairs, weight_grads, 0)

    for sub in range(per_group):
        total = part[col * per_group + sub]
        for dist in range(1, y_n):
            other = peer_y(dist)
            pltpu.make_async_remote_copy(
                src_ref=part.at[own], dst_ref=y_in.at[other, sub],
                send_sem=y_send.at[own], recv_sem=y_recv.at[other, sub],
                device_id=sibling, device_id_type=MESH,
            ).wait_recv()
            total = total + y_in[other, sub]
        gi_ref[sub * tokens:(sub + 1) * tokens, :] = total.astype(BF16)

    for t, step in enumerate([[(0, 0)]] + steps):
        for dh, dl in step:
            for chunk in range(CHUNKS):
                drain(dh, dl, chunk)
    for dist in range(1, y_n):
        x_to_y(dist).wait_send()
    for dist in range(y_n):
        x_to_sibling(dist).wait_send()

    def leave(block, carry):
        when(negate(mine(block)), lambda: pair_copy(block).wait_send())
        when(
            jnp.logical_and(mine(block), group_of(block) != col),
            lambda: y_copy(block).wait_send(),
        )
        return carry

    lax.fori_loop(0, rows, leave, 0)


def pick(coord_ref, gi_ref, blocks_ref, gi_out, gw_out):
    gi_out[...] = gi_ref[...]
    for s in range(gw_out.shape[0]):
        q = coord_ref[0, s]
        block = blocks_ref[jnp.maximum(q, 0)]
        gw_out[s] = jnp.where(q >= 0, block, jnp.zeros_like(block))


def solution(mesh):
    rows, cols = mesh.shape["row"], mesh.shape["col"]

    def local(x_act, grad_pre, weight_blocks, block_coord):
        blk = weight_blocks.shape[-1]
        slots = weight_blocks.shape[2]
        tokens, hidden = grad_pre.shape
        group, width = x_act.shape
        dma = pltpu.SemaphoreType.DMA
        y_n = cols // CORES
        anywhere = pl.BlockSpec(memory_space=pl.ANY)
        in_vmem = pl.BlockSpec(memory_space=pltpu.VMEM)
        grad_input, all_blocks = pl.pallas_call(
            functools.partial(kernel, rows, cols),
            out_shape=(
                jax.ShapeDtypeStruct((group, width), BF16),
                jax.ShapeDtypeStruct((width // blk * (hidden // blk), blk, blk), BF16),
            ),
            in_specs=[pl.BlockSpec(memory_space=pltpu.SMEM), anywhere, anywhere, anywhere],
            out_specs=(in_vmem, in_vmem),
            scratch_shapes=[
                pltpu.VMEM((rows, tokens, hidden), BF16),
                pltpu.VMEM((cols, group, width), BF16),
                pltpu.VMEM((width, cols * group), BF16),
                pltpu.VMEM((slots, blk, blk), BF16),
                pltpu.VMEM((slots, blk, blk), BF16),
                pltpu.VMEM((hidden, width), BF16),
                pltpu.VMEM((rows, tokens, width), F32),
                pltpu.VMEM((rows, tokens, width), F32),
                pltpu.VMEM((y_n, rows // cols, tokens, width), F32),
                dma((3,)),
                dma((4, rows, CHUNKS)),
                dma((rows, CHUNKS)),
                dma((2 * y_n,)),
                dma((cols,)),
                dma((rows,)),
                dma((rows,)),
                dma((rows,)),
                dma((y_n, rows // cols)),
            ],
            compiler_params=pltpu.CompilerParams(collective_id=0, has_side_effects=True),
        )(block_coord[0], x_act, grad_pre, weight_blocks.reshape(slots, blk, blk))
        grad_input, grad_weight = pl.pallas_call(
            pick,
            out_shape=(
                jax.ShapeDtypeStruct((group, width), BF16),
                jax.ShapeDtypeStruct((slots, blk, blk), BF16),
            ),
            in_specs=[pl.BlockSpec(memory_space=pltpu.SMEM), in_vmem, in_vmem],
            out_specs=(in_vmem, in_vmem),
        )(block_coord[0], grad_input, all_blocks)
        return grad_input, grad_weight.reshape(1, 1, slots, blk, blk)

    return jax.shard_map(
        local,
        mesh=mesh,
        in_specs=(
            P("col", "row"),
            P("row", "col"),
            P("row", "col", None, None, None),
            P("row", "col", None),
        ),
        out_specs=(P("col", "row"), P("row", "col", None, None, None)),
        check_vma=False,
    )
```

time: 105 us -> 39.7 us (0.38)
  waiting for transfers between devices: 66.1 us -> 0 us
  Pallas kernels: 0 us -> 38.9 us
  between operations: 14.2 us -> 0.64 us
  local copies, waits for them, and re-layouts: 11.8 us -> 0 us
  blocking collectives: 6.47 us -> 0 us
  matrix products: 3.79 us -> 0 us
  other arithmetic: 2.29 us -> 0 us
    all_gather x1 -> x0, waiting for transfers between devices: 53.3 us -> none  [local(): grad_slots = slots_of(lax.all_gather(grad_pre, 'row', axis=0, tiled=True))]
    pallas_call x0 -> x2, Pallas kernels: none -> 38.9 us  [the longest x1 36.6 us: local(): pl.pallas_call(functools.partial(kernel, rows, cols), out_shape=(jax.Shap...]
    reduce_scatter x1 -> x0, waiting for transfers between devices: 12.1 us -> none  [local(): lax.psum_scatter(x_partial, 'col', scatter_dimension=0, tiled=True)]
    all_gather x1 -> x0, blocking collectives: 6.47 us -> none  [local(): x_all = lax.all_gather(x_act, 'col', axis=0, tiled=True)]
    reshape x3 -> x0, local copies, waits for them, and re-layouts: 4.39 us -> none  [the longest x1 3.03 us: slots_of(): panel_rows.reshape(row_count, col_blocks, block_size)]
    all_gather x1 -> x0, local copies, waits for them, and re-layouts: 3.91 us -> none  [local(): grad_slots = slots_of(lax.all_gather(grad_pre, 'row', axis=0, tiled=True))]
    dot_general x2 -> x0, matrix products: 3.79 us -> none  [the longest x1 2.28 us: local(): jnp.einsum('nsb,rsab->nra', grad_slots, weights_by_row, preferred_element...]
    gather x2 -> x0, local copies, waits for them, and re-layouts: 2.8 us -> none  [the longest x1 1.95 us: slots_of(): jnp.take(panel_rows.reshape(row_count, col_blocks, block_size), block_col...]
  transfers between devices with their start and end apart: 2 -> 0, of which waited for: 2 -> 0; matrix products, arithmetic and copies ran while one was open for 3% -> 0% of each run, Pallas kernels for 0% -> 0%
where the time goes in v1:
time: 39.7 us; the launch traced here: 39.6 us
  Pallas kernels  38.9 us (98%)
  between operations  0.64 us (2%)
    pallas_call x1, Pallas kernels, local(): pl.pallas_call(functools.partial(kernel, rows, cols), out_shape=(jax.Shap...  36.6 us
    pallas_call x1, Pallas kernels, local(): pl.pallas_call(pick, out_shape=(jax.ShapeDtypeStruct((group, width), BF16...  2.33 us

profile of v1, /device:TPU:0, one launch (start us, length us, event | category | flops | bytes accessed | tf_op | source)
XLA Modules:
  0.0 39.6 jit_solution(11942520219518195574)
XLA Ops:
  0.6 36.6 %shard_map.59 = (bf16[128,384]{1,0:T(8,128)(2,1)}, bf16[48,128,128]{2,1,0:T(8,128)(2,1)}) custom-call(s32[1,12]{1,0:T(1,128)} %bitcast.4, bf16[128,384]{1,0:T(8,128)(2,1)} %x_ref.1, bf16[64,2048]{1,0:T(8,128)(2,1)} %g_ref.1, bf16[12,128,128]{2,1,0:T(8,128)(2,1)} %bitcast.3), custom_call_target="tpu_custom_call" | custom-call | tf_op jit(solution)/shard_map/pallas_call | solution.py:366
  37.2 2.3 %shard_map.60 = (bf16[128,384]{1,0:T(8,128)(2,1)}, bf16[12,128,128]{2,1,0:T(8,128)(2,1)}) custom-call(s32[1,12]{1,0:T(1,128)} %bitcast.5, bf16[128,384]{1,0:T(8,128)(2,1)} %get-tuple-element.6.gi_ref, bf16[48,128,128]{2,1,0:T(8,128)(2,1)} %get-tuple-element.7.blocks_ref), custom_call_target="tpu_custom_call" | custom-call | tf_op jit(solution)/shard_map/pallas_call | solution.py:396

commit v2 on v1

--- a/solution.py
+++ b/solution.py
@@ -46,8 +46,8 @@
 
 
 def kernel(
-    rows, cols, coord_ref, x_ref, g_ref, w_ref, gi_ref, gw_ref,
-    g_all, x_all, x_t, w_own, w_t, dense, part, pair_in, y_in,
+    rows, cols, coord_ref, x_ref, g_ref, w_ref, gi_ref, gw_out,
+    g_all, x_all, x_t, w_own, w_t, dense, part, pair_in, y_in, gw_ref,
     local_sem, g_send, g_recv, x_send, x_recv, pair_send, pair_recv, y_send, y_recv,
 ):
     hi_n = 4 if rows % 4 == 0 else 1
@@ -248,12 +248,6 @@
             dense[pl.ds(pl.multiple_of(c * blk, blk), blk), r * blk:(r + 1) * blk] = total
         return carry
 
-    lax.fori_loop(0, col_blocks, spread, 0)
-
-    own_g.wait()
-    own_x.wait()
-    compute(0, 0)
-
     steps = []
     for t in range(1, hi_n + lo_n - 1):
         step = []
@@ -266,31 +260,55 @@
                     step.append((dh, dl))
         steps.append(step)
 
-    pending = [(0, 0)]
+    def x_turn():
+        span = x_all.shape[1]
+        for dist in range(y_n):
+            x_from_sibling(dist).wait_recv()
+        for r in range(row_blocks):
+            for group in range(cols):
+                x_t[r * blk:(r + 1) * blk, group * span:(group + 1) * span] = x_all[
+                    group, :, r * blk:(r + 1) * blk
+                ].T
+
+    def arrivals(step, chunk):
+        for dh, dl in step:
+            arrive(dh, dl, chunk)
+
+    def computes(blocks):
+        for dh, dl in blocks:
+            compute(dh, dl)
+
+    def finishes(blocks):
+        for dh, dl in blocks:
+            finish(dh, dl)
+
+    lax.fori_loop(0, col_blocks // 2, spread, 0)
+    computed, waiting = [], [(0, 0)]
+    last = len(steps) - 1
     for index, step in enumerate(steps):
+        if index == last:
+            computes(waiting)
+            finishes(computed + waiting)
+            computed, waiting = [], []
+        cut = len(waiting) // 2
         for chunk in range(CHUNKS):
-            for dh, dl in step:
-                arrive(dh, dl, chunk)
+            arrivals(step, chunk)
+            if chunk == 0:
+                if index == 0:
+                    lax.fori_loop(col_blocks // 2, col_blocks, spread, 0)
+                    own_g.wait()
+                    own_x.wait()
+                computes(waiting[:cut])
+        computes(waiting[cut:])
+        finishes(computed)
+        computed, waiting = waiting, step
         if index == 0:
             for dist in range(1, y_n):
                 x_copy(0, peer_y(dist) * CORES + core, sibling).wait_recv()
                 x_to_sibling(dist).start()
-        for dh, dl in step:
-            compute(dh, dl)
-        if index < len(steps) - 1:
-            for dh, dl in pending:
-                finish(dh, dl)
-            pending = []
-        pending = pending + step
-        if index == min(1, len(steps) - 1):
-            for dist in range(y_n):
-                x_from_sibling(dist).wait_recv()
-            for r in range(row_blocks):
-                for group in range(cols):
-                    span = x_all.shape[1]
-                    x_t[r * blk:(r + 1) * blk, group * span:(group + 1) * span] = x_all[
-                        group, :, r * blk:(r + 1) * blk
-                    ].T
+        if index == min(1, last):
+            x_turn()
+    computes(waiting)
 
     pair_width = 2 * blk
 
@@ -306,10 +324,12 @@
         return carry
 
     pairs = col_blocks // 2
-    lax.fori_loop(0, pairs // 2, weight_grads, 0)
-    for dh, dl in pending:
-        finish(dh, dl)
-    lax.fori_loop(pairs // 2, pairs, weight_grads, 0)
+    early = pairs // 4
+    lax.fori_loop(0, early, weight_grads, 0)
+    finishes(computed + waiting)
+    lax.fori_loop(early, pairs, weight_grads, 0)
+    gw_copy = pltpu.make_async_copy(gw_ref, gw_out, local_sem.at[3])
+    gw_copy.start()
 
     for sub in range(per_group):
         total = part[col * per_group + sub]
@@ -341,14 +361,33 @@
         return carry
 
     lax.fori_loop(0, rows, leave, 0)
-
-
-def pick(coord_ref, gi_ref, blocks_ref, gi_out, gw_out):
+    gw_copy.wait()
+
+
+def pick(coord_ref, gi_ref, blocks_ref, gi_out, gw_out, held, into, out):
+    slots = held.shape[0]
+
+    def load(s):
+        return pltpu.make_async_copy(
+            blocks_ref.at[jnp.maximum(coord_ref[0, s], 0)], held.at[s], into.at[s]
+        )
+
+    def store(s):
+        return pltpu.make_async_copy(held.at[s], gw_out.at[s], out.at[s])
+
+    for s in range(slots):
+        load(s).start()
     gi_out[...] = gi_ref[...]
-    for s in range(gw_out.shape[0]):
-        q = coord_ref[0, s]
-        block = blocks_ref[jnp.maximum(q, 0)]
-        gw_out[s] = jnp.where(q >= 0, block, jnp.zeros_like(block))
+    for s in range(slots):
+        load(s).wait()
+
+        @pl.when(coord_ref[0, s] < 0)
+        def _():
+            held[s] = jnp.zeros(held.shape[1:], BF16)
+
+        store(s).start()
+    for s in range(slots):
+        store(s).wait()
 
 
 def solution(mesh):
@@ -370,7 +409,7 @@
                 jax.ShapeDtypeStruct((width // blk * (hidden // blk), blk, blk), BF16),
             ),
             in_specs=[pl.BlockSpec(memory_space=pltpu.SMEM), anywhere, anywhere, anywhere],
-            out_specs=(in_vmem, in_vmem),
+            out_specs=(in_vmem, anywhere),
             scratch_shapes=[
                 pltpu.VMEM((rows, tokens, hidden), BF16),
                 pltpu.VMEM((cols, group, width), BF16),
@@ -381,7 +420,8 @@
                 pltpu.VMEM((rows, tokens, width), F32),
                 pltpu.VMEM((rows, tokens, width), F32),
                 pltpu.VMEM((y_n, rows // cols, tokens, width), F32),
-                dma((3,)),
+                pltpu.VMEM((width // blk * (hidden // blk), blk, blk), BF16),
+                dma((4,)),
                 dma((4, rows, CHUNKS)),
                 dma((rows, CHUNKS)),
                 dma((2 * y_n,)),
@@ -399,8 +439,9 @@
                 jax.ShapeDtypeStruct((group, width), BF16),
                 jax.ShapeDtypeStruct((slots, blk, blk), BF16),
             ),
-            in_specs=[pl.BlockSpec(memory_space=pltpu.SMEM), in_vmem, in_vmem],
-            out_specs=(in_vmem, in_vmem),
+            in_specs=[pl.BlockSpec(memory_space=pltpu.SMEM), in_vmem, anywhere],
+            out_specs=(in_vmem, anywhere),
+            scratch_shapes=[pltpu.VMEM((slots, blk, blk), BF16), dma((slots,)), dma((slots,))],
         )(block_coord[0], grad_input, all_blocks)
         return grad_input, grad_weight.reshape(1, 1, slots, blk, blk)
 

time: 39.7 us -> 40.2 us (1.013); the launches traced: 39.6 us -> 39.6 us
    pallas_call x1, Pallas kernels: 36.6 us -> 35.6 us  [local(): pl.pallas_call(functools.partial(kernel, rows, cols), out_shape=(jax.Shap...]
    pallas_call x1, Pallas kernels: 2.33 us -> 3.32 us  [local(): pl.pallas_call(pick, out_shape=(jax.ShapeDtypeStruct((group, width), BF16...]
where the time goes in v2:
time: 40.2 us; the launch traced here: 39.6 us
  Pallas kernels  38.9 us (97%)
  between operations  0.64 us (2%)
    pallas_call x1, Pallas kernels, local(): pl.pallas_call(functools.partial(kernel, rows, cols), out_shape=(jax.Shap...  35.6 us
    pallas_call x1, Pallas kernels, local(): pl.pallas_call(pick, out_shape=(jax.ShapeDtypeStruct((group, width), BF16...  3.32 us

profile of v2, /device:TPU:0, one launch (start us, length us, event | category | flops | bytes accessed | tf_op | source)
XLA Modules:
  0.0 39.6 jit_solution(1993147856755139009)
XLA Ops:
  0.6 35.6 %shard_map.59 = (bf16[128,384]{1,0:T(8,128)(2,1)}, bf16[48,128,128]{2,1,0:T(8,128)(2,1)}) custom-call(s32[1,12]{1,0:T(1,128)} %bitcast.4, bf16[128,384]{1,0:T(8,128)(2,1)} %x_ref.1, bf16[64,2048]{1,0:T(8,128)(2,1)} %g_ref.1, bf16[12,128,128]{2,1,0:T(8,128)(2,1)} %bitcast.3), custom_call_target="tpu_custom_call" | custom-call | tf_op jit(solution)/shard_map/pallas_call | solution.py:405
  36.2 3.3 %shard_map.60 = (bf16[128,384]{1,0:T(8,128)(2,1)}, bf16[12,128,128]{2,1,0:T(8,128)(2,1)}) custom-call(s32[1,12]{1,0:T(1,128)} %bitcast.5, bf16[128,384]{1,0:T(8,128)(2,1)} %get-tuple-element.6.gi_ref, bf16[48,128,128]{2,1,0:T(8,128)(2,1)} %get-tuple-element.7.blocks_ref), custom_call_target="tpu_custom_call" | custom-call | tf_op jit(solution)/shard_map/pallas_call | solution.py:436
